TPU v7x, 256 devices: a whole 4x4x8 slice. The times are simulated.
256 devices in a mesh: row: 16 (over y, x), col: 16 (over z, core).
Axes of the slice: x: 4, y: 4, z: 8, core: 2. Of those that a mesh axis runs over, the one named last changes fastest.
Arguments:
- matrix: float32 [16384, 16384], P('row', 'col'), may hold values from 0 to 9.5, as said below
Outputs:
- factored: float32 [16384, 16384], P('row', 'col')
Inputs may be any that keep to these rules, and one draw needn't show every extreme that they name: `matrix`: symmetric positive definite once the block order is reverted.
All inputs are finite; a program needn't handle non-finite values.
Results may differ from a plain program's by a relative error of at most 0.0003.
Values sent between devices are 32-bit elements; how exact they have to be, the bound alone decides.
A program may use at most 128 MiB of HBM per device.

v0:
```python
import jax
import jax.numpy as jnp
from jax import lax
from jax.sharding import PartitionSpec as P

NB = 256
PANELS = 3


def from_root(shard, axis, root):
    mine = lax.axis_index(axis) == root
    return lax.psum(jnp.where(mine, shard, jnp.zeros_like(shard)), axis)


def solve_panel(factor, raw_rows):
    slots = raw_rows.shape[0]
    width = raw_rows.shape[1]
    flat = raw_rows.reshape(slots * width, width)
    solved = jax.scipy.linalg.solve_triangular(factor, flat.T, lower=True).T
    return solved.reshape(slots, width, width)


def subtract(part, panel_rows, column_rows):
    return part - jnp.einsum(
        "lan,mbn->lamb",
        panel_rows,
        column_rows,
        precision=lax.Precision.HIGHEST,
        preferred_element_type=jnp.float32,
    )


def body(matrix):
    grid_rows = lax.axis_size("row")
    grid_cols = lax.axis_size("col")
    row_slots = matrix.shape[0] // NB
    col_slots = matrix.shape[1] // NB
    stride = grid_cols // grid_rows
    my_row = lax.axis_index("row")
    my_col = lax.axis_index("col")
    blocks = matrix.reshape(row_slots, NB, col_slots, NB)
    row_ids = jnp.arange(row_slots, dtype=jnp.int32) * grid_rows + my_row
    col_ids = jnp.arange(col_slots, dtype=jnp.int32) * grid_cols + my_col
    carried = None
    for panel_at in range(PANELS):
        root_row = panel_at % grid_rows
        root_col = panel_at % grid_cols
        slot_row = panel_at // grid_rows
        slot_col = panel_at // grid_cols
        source = blocks[:, :, slot_col, :]
        below_mask = (row_ids > panel_at)[:, None, None]
        diag_block = from_root(source[slot_row], "row", root_row)
        factor = jnp.linalg.cholesky(diag_block)
        solved = jnp.where(below_mask, solve_panel(factor, source), 0.0)
        panel_rows = from_root(solved, "col", root_col)
        fetched = from_root(panel_rows, "row", my_col % grid_rows)
        column_rows = lax.dynamic_index_in_dim(
            fetched.reshape(col_slots, stride, NB, NB), my_col // grid_rows, 1, keepdims=False
        )
        owner_column = jnp.where((row_ids == panel_at)[:, None, None], factor[None], panel_rows)
        blocks = blocks.at[:, :, slot_col, :].set(
            jnp.where(my_col == root_col, owner_column, source)
        )
        blocks = subtract(blocks, panel_rows, column_rows)
        carried = None
    zero_mask = (row_ids[:, None] < col_ids[None, :]) & (row_ids[:, None] < PANELS)
    result = jnp.where(zero_mask[:, None, :, None], 0.0, blocks)
    return result.reshape(matrix.shape)


def solution(mesh):
    in_specs = (P("row", "col"),)
    out_specs = P("row", "col")
    return jax.shard_map(body, mesh=mesh, in_specs=in_specs, out_specs=out_specs, check_vma=False)
```

profile of v0, /device:TPU:1, one launch (start us, length us, event | category | flops | bytes accessed | tf_op | source)
XLA Modules:
  0.0 1180.2 jit_solution(10339150950592994072)
XLA Ops:
  6.5 5.6 reshape.239
  12.1 5.2 copy.29
  17.4 1.7 fusion.18
  19.1 2.9 slice.154
  22.2 93.9 %all-reduce.11.cloned.1.call-done = f32[256,256]{0,1:T(8,128)} async-done(((f32[256,256]{0,1:T(8,128)}), f32[256,256]{0,1:T(8,128)}) %all-reduce.11.cloned.1.call-update) | async-done | bytes 262160 | tf_op jit(solution)/shard_map/psum | solution.py:12
  118.1 11.7 cholesky.172
  129.9 9.8 custom-call.15
  140.2 11.7 cholesky.189
  154.0 4.2 while.9
  154.8 1.4 bitcast_dynamic-update-slice_fusion.7
  156.8 1.4 bitcast_dynamic-update-slice_fusion.7
  158.2 19.7 %custom-call.16 = f32[2,128,128]{1,2,0:T(8,128)S(1)} custom-call(f32[2,128,128]{2,1,0:T(8,128)S(1)} %get-tuple-element.63), custom_call_target="InvertDiagBlocksLowerTriangular" | custom-call | tf_op jit(solution)/shard_map/jit(_solve_triangular)/triangular_solve | solution.py:19
  182.2 112.0 %all-reduce.13.cloned.1.call-done = f32[4,256,256]{1,2,0:T(8,128)} async-done(((f32[4,256,256]{1,2,0:T(8,128)}), f32[4,256,256]{1,2,0:T(8,128)}) %all-reduce.13.cloned.1.call-update) | async-done | bytes 1048592 | tf_op jit(solution)/shard_map/psum | solution.py:12
  296.2 1.2 bitcast_dynamic-update-slice_fusion.3
  297.4 96.2 %all-reduce.15.cloned.1.call-done = f32[4,256,256]{1,2,0:T(8,128)} async-done(((f32[4,256,256]{1,2,0:T(8,128)}), f32[4,256,256]{1,2,0:T(8,128)}) %all-reduce.15.cloned.1.call-update) | async-done | bytes 1048592 | tf_op jit(solution)/shard_map/psum | solution.py:12
  393.6 5.8 convolution_subtract_fusion.1
  399.4 2.0 copy-done.1
  402.6 1.4 slice_bitcast_fusion.1
  404.4 91.7 %all-reduce.17.cloned.1.call-done = f32[256,256]{0,1:T(8,128)} async-done(((f32[256,256]{0,1:T(8,128)}), f32[256,256]{0,1:T(8,128)}) %all-reduce.17.cloned.1.call-update) | async-done | bytes 262160 | tf_op jit(solution)/shard_map/psum | solution.py:12
  498.2 11.7 cholesky.206
  509.9 9.8 custom-call.17
  520.2 11.7 cholesky.223
  534.6 4.2 while.10
  535.5 1.3 bitcast_dynamic-update-slice_fusion.8
  537.5 1.3 bitcast_dynamic-update-slice_fusion.8
  538.9 19.7 %custom-call.18 = f32[2,128,128]{1,2,0:T(8,128)S(1)} custom-call(f32[2,128,128]{2,1,0:T(8,128)S(1)} %get-tuple-element.64), custom_call_target="InvertDiagBlocksLowerTriangular" | custom-call | tf_op jit(solution)/shard_map/jit(_solve_triangular)/triangular_solve | solution.py:19
  561.7 1.2 select_select_fusion.1
  563.0 112.0 %all-reduce.19.cloned.1.call-done = f32[4,256,256]{1,2,0:T(8,128)} async-done(((f32[4,256,256]{1,2,0:T(8,128)}), f32[4,256,256]{1,2,0:T(8,128)}) %all-reduce.19.cloned.1.call-update) | async-done | bytes 1048592 | tf_op jit(solution)/shard_map/psum | solution.py:12
  676.6 1.2 fusion.3
  677.8 96.4 %all-reduce.21.cloned.1.call-done = f32[4,256,256]{1,2,0:T(8,128)} async-done(((f32[4,256,256]{1,2,0:T(8,128)}), f32[4,256,256]{1,2,0:T(8,128)}) %all-reduce.21.cloned.1.call-update) | async-done | bytes 1048592 | tf_op jit(solution)/shard_map/psum | solution.py:12
  774.2 5.8 convolution_subtract_fusion
  780.0 2.0 copy-done
  783.1 1.4 slice_bitcast_fusion
  784.8 92.0 %all-reduce.23.cloned.1.call-done = f32[256,256]{0,1:T(8,128)} async-done(((f32[256,256]{0,1:T(8,128)}), f32[256,256]{0,1:T(8,128)}) %all-reduce.23.cloned.1.call-update) | async-done | bytes 262160 | tf_op jit(solution)/shard_map/psum | solution.py:12
  878.9 11.7 cholesky.240
  890.6 9.8 custom-call.19
  900.9 11.7 cholesky.257
  915.4 4.3 while.11
  916.3 1.3 bitcast_dynamic-update-slice_fusion.9
  918.3 1.3 bitcast_dynamic-update-slice_fusion.9
  919.7 19.7 %custom-call.20 = f32[2,128,128]{1,2,0:T(8,128)S(1)} custom-call(f32[2,128,128]{2,1,0:T(8,128)S(1)} %get-tuple-element.65), custom_call_target="InvertDiagBlocksLowerTriangular" | custom-call | tf_op jit(solution)/shard_map/jit(_solve_triangular)/triangular_solve | solution.py:19
  942.5 1.2 select_select_fusion
  943.8 112.2 %all-reduce.25.cloned.1.call-done = f32[4,256,256]{1,2,0:T(8,128)} async-done(((f32[4,256,256]{1,2,0:T(8,128)}), f32[4,256,256]{1,2,0:T(8,128)}) %all-reduce.25.cloned.1.call-update) | async-done | bytes 1048592 | tf_op jit(solution)/shard_map/psum | solution.py:12
  1057.6 1.2 fusion.1
  1058.7 96.6 %all-reduce.27.cloned.1.call-done = f32[4,256,256]{1,2,0:T(8,128)} async-done(((f32[4,256,256]{1,2,0:T(8,128)}), f32[4,256,256]{1,2,0:T(8,128)}) %all-reduce.27.cloned.1.call-update) | async-done | bytes 1048592 | tf_op jit(solution)/shard_map/psum | solution.py:12
  1155.3 7.5 subtract_select_fusion
  1162.8 5.2 copy.53
  1168.0 5.2 copy.76
  (115 shorter events, 33.8 us)
Async XLA Ops:
  6.5 109.5 %all-reduce.11.cloned.1.call-start = ((), (), s32[]{:S(2)}) async-start(), calls=%async_computation | async-start | bytes 524288 | tf_op jit(solution)/shard_map/psum | solution.py:12
  19.1 275.1 %all-reduce.13.cloned.1.call-start = ((), (), s32[]{:S(2)}) async-start(), calls=%async_computation.1 | async-start | bytes 2097152 | tf_op jit(solution)/shard_map/psum | solution.py:12
  182.1 211.5 %all-reduce.15.cloned.1.call-start = ((), (), s32[]{:S(2)}) async-start(), calls=%async_computation.2 | async-start | bytes 2097152 | tf_op jit(solution)/shard_map/psum | solution.py:12
  294.2 2.0 copy-start.2
  295.3 200.8 %all-reduce.17.cloned.1.call-start = ((), (), s32[]{:S(2)}) async-start(), calls=%async_computation.3 | async-start | bytes 524288 | tf_op jit(solution)/shard_map/psum | solution.py:12
  399.4 2.0 copy-start.1
  402.2 272.8 %all-reduce.19.cloned.1.call-start = ((), (), s32[]{:S(2)}) async-start(), calls=%async_computation.4 | async-start | bytes 2097152 | tf_op jit(solution)/shard_map/psum | solution.py:12
  562.9 211.3 %all-reduce.21.cloned.1.call-start = ((), (), s32[]{:S(2)}) async-start(), calls=%async_computation.5 | async-start | bytes 2097152 | tf_op jit(solution)/shard_map/psum | solution.py:12
  675.0 1.6 copy-start.3
  676.1 200.7 %all-reduce.23.cloned.1.call-start = ((), (), s32[]{:S(2)}) async-start(), calls=%async_computation.6 | async-start | bytes 524288 | tf_op jit(solution)/shard_map/psum | solution.py:12
  780.0 2.0 copy-start
  782.8 273.2 %all-reduce.25.cloned.1.call-start = ((), (), s32[]{:S(2)}) async-start(), calls=%async_computation.7 | async-start | bytes 2097152 | tf_op jit(solution)/shard_map/psum | solution.py:12
  943.7 211.6 %all-reduce.27.cloned.1.call-start = ((), (), s32[]{:S(2)}) async-start(), calls=%async_computation.8 | async-start | bytes 2097152 | tf_op jit(solution)/shard_map/psum | solution.py:12
  1055.9 1.6 copy-start.4
Sparse Core Ops, SparseCore 0:
  19.2 96.8 all-reduce.10
  182.2 111.9 all-reduce.12
  297.5 96.0 all-reduce.14
  402.3 93.7 all-reduce.16
  563.0 111.8 all-reduce.18
  678.1 96.0 all-reduce.20
  782.9 93.8 all-reduce.22
  943.8 112.0 all-reduce.24
  1059.2 96.0 all-reduce.26
where the time goes:
time: 1190 us; the launch traced here: 1180 us
  waiting for transfers between devices  903 us (76%)
  other arithmetic  179 us (15%)
  local copies, waits for them, and re-layouts  50.7 us (4%)
  matrix products  27.3 us (2%)
  between operations  18 us (2%)
    psum x9, waiting for transfers between devices, from_root(): return lax.psum(jnp.where(mine, shard, jnp.zeros_like(shard)), axis)  903 us
    another operation x20, other arithmetic, body(): factor = jnp.linalg.cholesky(diag_block)  103 us
    another operation x7, other arithmetic, solve_panel(): solved = jax.scipy.linalg.solve_triangular(factor, flat.T, lower=True).T  59.1 us
  transfers between devices with their start and end apart: 9, of which 9 were waited for; matrix products, arithmetic and copies ran while one was open for 1% of the time, Pallas kernels for 0%

commit v1 on v0

v1 whole, which is shorter than its diff:
```python
import functools

import jax
import jax.numpy as jnp
from jax import lax
from jax.experimental import pallas as pl
from jax.experimental.pallas import tpu as pltpu
from jax.sharding import PartitionSpec as P

NB = 256
PANELS = 3
LEAF = 32
MESH = pl.DeviceIdType.MESH
F32 = jnp.float32
BF16 = jnp.bfloat16


def split2(x):
    hi = x.astype(BF16)
    return hi, (x - hi.astype(F32)).astype(BF16)


def split3(x):
    hi = x.astype(BF16)
    rest = x - hi.astype(F32)
    mid = rest.astype(BF16)
    return hi, mid, (rest - mid.astype(F32)).astype(BF16)


def dot_split(a, b, dims):
    d = functools.partial(lax.dot_general, dimension_numbers=(dims, ((), ())), preferred_element_type=F32)
    return d(a[0], b[0]) + (d(a[0], b[1]) + d(a[1], b[0]))


def dot_full(a, b, dims):
    return lax.dot_general(a, b, (dims, ((), ())), precision=lax.Precision.HIGHEST, preferred_element_type=F32)


NN = ((1,), (0,))
NT = ((1,), (1,))
TN = ((0,), (0,))


def factor_panel(work, hooks):
    strips = LEAF // 8
    sub = lax.broadcasted_iota(jnp.int32, (8, 128), 0)
    for leaf in range(NB // LEAF):
        top = leaf * LEAF
        end = top + LEAF
        tiles = [q for q in range(2) if (q + 1) * 128 > top] + [2 + q for q in range(2) if q * 128 < end]
        rows = {
            (t, q): work[top + 8 * t : top + 8 * t + 8, q * 128 : (q + 1) * 128] for t in range(strips) for q in tiles
        }
        for s in range(strips):
            first = top + 8 * s
            q0, at = first // 128, first % 128
            cols = {
                (i, t): jnp.broadcast_to(rows[t, q0][:, at + i : at + i + 1], (8, 128))
                for i in range(8)
                for t in range(s, strips)
            }
            scales = None
            for i in range(8):
                r = lax.rsqrt(jnp.broadcast_to(cols[i, s][i : i + 1, :], (8, 128)))
                scales = r if scales is None else jnp.where(sub == i, r, scales)
                low = {t: cols[i, t] * r for t in range(s, strips)}
                low[s] = jnp.where(sub > i, low[s], 0.0)
                left = range(s + 1 if i == 7 else s, strips)
                for other in range(i + 1, 8):
                    pivot = jnp.broadcast_to(cols[other, s][i : i + 1, :], (8, 128)) * r
                    for t in left:
                        cols[other, t] = cols[other, t] - low[t] * pivot
                for q in tiles:
                    pivot = jnp.broadcast_to(rows[s, q][i : i + 1, :], (8, 128)) * r
                    for t in left:
                        rows[t, q] = rows[t, q] - low[t] * pivot
            for q in tiles:
                work[first : first + 8, q * 128 : (q + 1) * 128] = rows[s, q] * scales
        if end < NB:
            lo, hi = tiles[0] * 128, (tiles[-1] + 1) * 128
            h, m, l = split3(work[top:end, lo:hi])
            rhs = jnp.concatenate([h, m, h, l, m, h], axis=0)
            lhs = jnp.concatenate([v[:, : NB - lo] for v in (h, h, m, h, m, l)], axis=0)
            prod = lax.dot_general(lhs, rhs, (TN, ((), ())), preferred_element_type=F32)
            work[end:, lo:hi] = work[end:, lo:hi] - prod[end - lo :, :]
        if leaf in hooks:
            hooks[leaf]()


def kernel(
    mat, out, held, aj, a11, ai, uj_hi, uj_lo, li_hi, li_lo, urow, work,
    local_sem,
    s_sj, s_si, s_z, s_ax, s_ay, s_j1, s_j2, s_iz, s_ic,
    r_sj, r_si, r_z, r_ax, r_ay, r_j1, r_j2, r_iz, r_ic,
):
    row = lax.axis_index("row")
    col = lax.axis_index("col")
    y, x = row // 4, row % 4
    z, core = col // 2, col % 2

    def copy(src, dst, send, recv, **dev):
        return pltpu.make_async_remote_copy(
            src_ref=src, dst_ref=dst, send_sem=send, recv_sem=recv, device_id=dev, device_id_type=MESH
        )

    barrier = pltpu.get_barrier_semaphore()

    def greet(d, carry):
        pl.semaphore_signal(barrier, inc=1, device_id={"row": (row + d) % 16}, device_id_type=MESH)
        pl.semaphore_signal(barrier, inc=1, device_id={"col": (col + d) % 16}, device_id_type=MESH)
        return carry

    lax.fori_loop(1, 16, greet, 0)
    load = pltpu.make_async_copy(mat, held, local_sem.at[0])
    load.start()
    pl.semaphore_wait(barrier, 30)

    def scatter_j(d):
        p = (row + d) % 16
        return copy(
            mat.at[pl.ds(16 * p, 16), :], aj.at[p // 4, p % 4, row], s_sj.at[d], r_sj.at[row], row=p
        )

    def scatter_i(d):
        p = (col + d) % 16
        return copy(
            mat.at[pl.ds(64 * p, 64), pl.ds(0, NB)], ai.at[p // 2, p % 2, col], s_si.at[d], r_si.at[col], col=p
        )

    def loop(n0, n1, body):
        def step(d, carry):
            body(d)
            return carry

        lax.fori_loop(n0, n1, step, 0)

    @pl.when(row < PANELS)
    def _():
        pltpu.make_async_copy(mat.at[pl.ds(16 * row, 16), :], aj.at[y, x, row], r_sj.at[row]).start()
        loop(1, 16, lambda d: scatter_j(d).start())

    @pl.when(col < PANELS)
    def _():
        pltpu.make_async_copy(
            mat.at[pl.ds(64 * col, 64), pl.ds(0, NB)], ai.at[z, core, col], r_si.at[col]
        ).start()
        loop(1, 16, lambda d: scatter_i(d).start())

    for k in range(PANELS):
        pltpu.make_async_copy(aj.at[y, x, k], aj.at[y, x, k], r_sj.at[k]).wait()

    def spread(k, d):
        return copy(
            aj.at[y, x, k, :, pl.ds(0, NB)],
            a11.at[y, x, k, :, pl.ds(pl.multiple_of(NB * col, NB), NB)],
            s_z.at[k, d], r_z.at[k, col], col=(col + d) % 16,
        )

    for k in range(PANELS):
        @pl.when((col < PANELS) & (col >= k))
        def _():
            pltpu.make_async_copy(
                aj.at[y, x, k, :, pl.ds(0, NB)],
                a11.at[y, x, k, :, pl.ds(pl.multiple_of(NB * col, NB), NB)],
                r_z.at[k, col],
            ).start()
            loop(1, 16, lambda d: spread(k, d).start())

    HALF = 512

    def j_first_x(d):
        return copy(
            aj.at[y, x, :, :, pl.ds(0, HALF)], aj.at[y, x, :, :, pl.ds(0, HALF)],
            s_j1.at[0, d], r_j1.at[0, x], row=y * 4 + (x + d) % 4,
        )

    def j_first_y(d):
        return copy(
            aj.at[y, x, :, :, pl.ds(HALF, HALF)], aj.at[y, x, :, :, pl.ds(HALF, HALF)],
            s_j1.at[1, d], r_j1.at[1, y], row=((y + d) % 4) * 4 + x,
        )

    def j_then_y(d):
        return copy(
            aj.at[y, :, :, :, pl.ds(0, HALF)], aj.at[y, :, :, :, pl.ds(0, HALF)],
            s_j2.at[0, d], r_j2.at[0, y], row=((y + d) % 4) * 4 + x,
        )

    def j_then_x(d):
        return copy(
            aj.at[:, x, :, :, pl.ds(HALF, HALF)], aj.at[:, x, :, :, pl.ds(HALF, HALF)],
            s_j2.at[1, d], r_j2.at[1, x], row=y * 4 + (x + d) % 4,
        )

    def a_x(k, d):
        ref = a11.at[y, x, k, :, pl.ds(NB * k, NB * (PANELS - k))]
        return copy(ref, ref, s_ax.at[k, d], r_ax.at[k, x], row=y * 4 + (x + d) % 4)

    def a_y(k, d):
        ref = a11.at[y, :, k, :, pl.ds(NB * k, NB * (PANELS - k))]
        return copy(ref, ref, s_ay.at[k, d], r_ay.at[k, y], row=((y + d) % 4) * 4 + x)

    def wait_here(ref, sem):
        pltpu.make_async_copy(ref, ref, sem).wait()

    for k in range(PANELS):
        for j in range(k, PANELS):
            wait_here(a11.at[y, x, k, :, pl.ds(NB * j, NB)], r_z.at[k, j])
        loop(1, 4, lambda d: a_x(k, d).start())
    for k in range(PANELS):
        for d in range(1, 4):
            src = (x + d) % 4
            wait_here(a11.at[y, src, k, :, pl.ds(NB * k, NB * (PANELS - k))], r_ax.at[k, src])
        loop(1, 4, lambda d: a_y(k, d).start())
        if k == 0:
            loop(1, 4, lambda d: j_first_x(d).start())
            loop(1, 4, lambda d: j_first_y(d).start())

    def i_ring(d):
        return copy(
            ai.at[z, core], ai.at[z, core], s_iz.at[d], r_iz.at[z], col=((z + d) % 8) * 2 + core
        )

    def i_core(src):
        return copy(
            ai.at[src, core], ai.at[src, core], s_ic.at[src], r_ic.at[src], col=z * 2 + 1 - core
        )

    for k in range(PANELS):
        wait_here(ai.at[z, core, k], r_si.at[k])
    loop(1, 8, lambda d: i_ring(d).start())
    i_core(z).start()

    def wait_a11(k):
        for d in range(1, 4):
            src = (y + d) % 4
            wait_here(a11.at[src, :, k, :, pl.ds(NB * k, NB * (PANELS - k))], r_ay.at[k, src])

    def forward_j():
        for d in range(1, 4):
            src = (x + d) % 4
            wait_here(aj.at[y, src, :, :, pl.ds(0, HALF)], r_j1.at[0, src])
        loop(1, 4, lambda d: j_then_y(d).start())
        for d in range(1, 4):
            src = (y + d) % 4
            wait_here(aj.at[src, x, :, :, pl.ds(HALF, HALF)], r_j1.at[1, src])
        loop(1, 4, lambda d: j_then_x(d).start())

    def forward_i():
        def step(d):
            src = (z + d) % 8
            wait_here(ai.at[src, core], r_iz.at[src])
            i_core(src).start()

        loop(1, 8, step)

    def finish_bulk():
        for d in range(1, 4):
            src = (y + d) % 4
            wait_here(aj.at[src, :, :, :, pl.ds(0, HALF)], r_j2.at[0, src])
        for d in range(1, 4):
            src = (x + d) % 4
            wait_here(aj.at[:, src, :, :, pl.ds(HALF, HALF)], r_j2.at[1, src])
        loop(0, 8, lambda src: wait_here(ai.at[src, 1 - core], r_ic.at[src]))

    eye = (
        lax.broadcasted_iota(jnp.int32, (NB, NB), 0) == lax.broadcasted_iota(jnp.int32, (NB, NB), 1)
    ).astype(F32)
    for k in range(PANELS):
        wait_a11(k)
        lo = NB * k
        diag = a11[:, :, k, :, lo : lo + NB].reshape(NB, NB)
        for kk in range(k):
            u = urow[kk, :, lo - NB : lo]
            diag = diag - dot_full(u, u, TN)
        work[:, :NB] = diag
        work[:, NB:] = eye
        factor_panel(work, {0: forward_j, 4: forward_i} if k == 0 else {})
        inv = work[:, NB:]
        inv2 = split2(inv)
        if k < PANELS - 1:
            rest = a11[:, :, k, :, lo + NB :].reshape(NB, -1)
            for kk in range(k):
                rest = rest - dot_full(urow[kk, :, lo - NB : lo], urow[kk, :, lo:], TN)
            urow[k, :, lo : 2 * NB] = dot_full(inv, rest, NN)
        if k == 0:
            finish_bulk()
        for ch in range(4):
            at = slice(NB * ch, NB * ch + NB)
            rhs = aj[:, :, k, :, at].reshape(NB, NB)
            lhs = ai[2 * ch : 2 * ch + 2, :, k].reshape(NB, NB)
            for kk in range(k):
                u2 = split2(urow[kk, :, lo - NB : lo])
                rhs = rhs - dot_split(u2, (uj_hi[kk, :, at], uj_lo[kk, :, at]), TN)
                lhs = lhs - dot_split((li_hi[kk, at], li_lo[kk, at]), u2, NN)
            hi, low = split2(dot_split(inv2, split2(rhs), NN))
            uj_hi[k, :, at] = hi
            uj_lo[k, :, at] = low
            full = dot_split(split2(lhs), inv2, NT)
            hi, low = split2(full)
            li_hi[k, at] = hi
            li_lo[k, at] = low

    load.wait()

    for ch in range(4):
        at = slice(NB * ch, NB * ch + NB)
        for cc in range(4):
            to = slice(NB * cc, NB * cc + NB)
            total = held[at, to]
            for k in range(PANELS):
                total = total - dot_split((li_hi[k, at], li_lo[k, at]), (uj_hi[k, :, to], uj_lo[k, :, to]), NN)
            held[at, to] = total

    @pl.when(row < PANELS)
    def _():
        held[:NB, :] = jnp.zeros((NB, 4 * NB), F32)

    rr = lax.broadcasted_iota(jnp.int32, (NB, NB), 0)
    cc = lax.broadcasted_iota(jnp.int32, (NB, NB), 1)
    for k in range(PANELS):
        @pl.when(col == k)
        def _():
            first = li_hi[k, :NB].astype(F32) + li_lo[k, :NB].astype(F32)
            keep = (row > k) | ((row == k) & (rr >= cc))
            held[:NB, :NB] = jnp.where(keep, first, 0.0)
            held[NB:, :NB] = li_hi[k, NB:].astype(F32) + li_lo[k, NB:].astype(F32)

    store = pltpu.make_async_copy(held, out, local_sem.at[1])
    store.start()

    @pl.when(row < PANELS)
    def _():
        loop(1, 16, lambda d: scatter_j(d).wait_send())

    @pl.when(col < PANELS)
    def _():
        loop(1, 16, lambda d: scatter_i(d).wait_send())

    for k in range(PANELS):
        @pl.when((col < PANELS) & (col >= k))
        def _():
            loop(1, 16, lambda d: spread(k, d).wait_send())

        loop(1, 4, lambda d: a_x(k, d).wait_send())
        loop(1, 4, lambda d: a_y(k, d).wait_send())
    for c in (j_first_x, j_first_y, j_then_y, j_then_x):
        loop(1, 4, lambda d: c(d).wait_send())
    loop(1, 8, lambda d: i_ring(d).wait_send())
    loop(0, 8, lambda d: i_core(d).wait_send())
    store.wait()


def body(matrix):
    rows = matrix.shape[0]
    dma = pltpu.SemaphoreType.DMA
    groups = [(16,), (16,), (3, 16), (3, 4), (3, 4), (2, 4), (2, 4), (8,), (8,)]
    landed = [(3,), (3,), (3, 3), (3, 4), (3, 4), (2, 4), (2, 4), (8,), (8,)]
    return pl.pallas_call(
        kernel,
        out_shape=jax.ShapeDtypeStruct(matrix.shape, F32),
        in_specs=[pl.BlockSpec(memory_space=pl.ANY)],
        out_specs=pl.BlockSpec(memory_space=pl.ANY),
        scratch_shapes=[
            pltpu.VMEM(matrix.shape, F32),
            pltpu.VMEM((4, 4, PANELS, 16, rows), F32),
            pltpu.VMEM((4, 4, PANELS, 16, PANELS * NB), F32),
            pltpu.VMEM((8, 2, PANELS, 64, NB), F32),
            pltpu.VMEM((PANELS, NB, rows), BF16),
            pltpu.VMEM((PANELS, NB, rows), BF16),
            pltpu.VMEM((PANELS, rows, NB), BF16),
            pltpu.VMEM((PANELS, rows, NB), BF16),
            pltpu.VMEM((PANELS - 1, NB, (PANELS - 1) * NB), F32),
            pltpu.VMEM((NB, 2 * NB), F32),
            dma((2,)),
        ]
        + [dma(g) for g in groups]
        + [dma(g) for g in landed],
        compiler_params=pltpu.CompilerParams(
            collective_id=0, has_side_effects=True, vmem_limit_bytes=56 * 1024 * 1024
        ),
    )(matrix)


def solution(mesh):
    return jax.shard_map(body, mesh=mesh, in_specs=(P("row", "col"),), out_specs=P("row", "col"), check_vma=False)
```

time: 1190 us -> 115 us (0.10)
  waiting for transfers between devices: 903 us -> 0 us
  other arithmetic: 179 us -> 0 us
  Pallas kernels: 0 us -> 109 us
  local copies, waits for them, and re-layouts: 50.7 us -> 4.79 us
  matrix products: 27.3 us -> 0 us
  between operations: 18 us -> 0.01 us
    psum x9 -> x0, waiting for transfers between devices: 903 us -> none  [from_root(): return lax.psum(jnp.where(mine, shard, jnp.zeros_like(shard)), axis)]
    another operation x27 -> x0, other arithmetic: 162 us -> none  [the longest x20 103 us: body(): factor = jnp.linalg.cholesky(diag_block)]
    pallas_call x0 -> x1, Pallas kernels: none -> 109 us  [body(): pl.pallas_call(kernel, out_shape=jax.ShapeDtypeStruct(matrix.shape, F32),...]
    dot_general x3 -> x0, matrix products: 19.1 us -> none  [subtract(): jnp.einsum('lan,mbn->lamb', panel_rows, column_rows, precision=lax.Precis...]
    another operation x28 -> x0, local copies, waits for them, and re-layouts: 12.1 us -> none  [the longest x22 12 us: solve_panel(): solved = jax.scipy.linalg.solve_triangular(factor, flat.T, lower=True).T]
  transfers between devices with their start and end apart: 9 -> 0, of which waited for: 9 -> 0; matrix products, arithmetic and copies ran while one was open for 1% -> 0% of each run, Pallas kernels for 0% -> 0%
where the time goes in v1:
time: 115 us; the launch traced here: 114 us
  Pallas kernels  109 us (95%)
  local copies, waits for them, and re-layouts  4.79 us (4%)
    pallas_call x1, Pallas kernels, body(): pl.pallas_call(kernel, out_shape=jax.ShapeDtypeStruct(matrix.shape, F32),...  109 us
    unnamed x1, local copies, waits for them, and re-layouts  4.79 us

profile of v1, /device:TPU:1, one launch (start us, length us, event | category | flops | bytes accessed | tf_op | source)
XLA Modules:
  0.0 113.7 jit_solution(17653328921146810111)
XLA Ops:
  0.0 108.9 %shard_map.17 = f32[1024,1024]{1,0:T(8,128)} custom-call(f32[1024,1024]{1,0:T(8,128)} %mat.1), custom_call_target="tpu_custom_call" | custom-call | tf_op jit(solution)/shard_map/pallas_call | solution.py:359
  108.9 4.8 %copy.3 = f32[1024,1024]{1,0:T(8,128)} copy(f32[1024,1024]{1,0:T(8,128)} %shard_map.17) | data formatting | bytes 8388608

commit v2 on v1

v2 whole, which is shorter than its diff:
```python
import functools

import jax
import jax.numpy as jnp
from jax import lax
from jax.experimental import pallas as pl
from jax.experimental.pallas import tpu as pltpu
from jax.sharding import PartitionSpec as P

NB = 256
PANELS = 3
LEAF = 32
MESH = pl.DeviceIdType.MESH
F32 = jnp.float32
BF16 = jnp.bfloat16


LEFT = (0, 0, 1, 0, 1, 2)
RIGHT = (0, 1, 0, 2, 1, 0)


def split3(x):
    hi = x.astype(BF16)
    rest = x - hi.astype(F32)
    mid = rest.astype(BF16)
    return hi, mid, (rest - mid.astype(F32)).astype(BF16)


def dot_parts(a, b, dims):
    lhs = jnp.concatenate([a[i] for i in LEFT], axis=dims[0][0])
    rhs = jnp.concatenate([b[i] for i in RIGHT], axis=dims[1][0])
    return lax.dot_general(lhs, rhs, (dims, ((), ())), preferred_element_type=F32)


NN = ((1,), (0,))
NT = ((1,), (1,))
TN = ((0,), (0,))
FIRST = (0, 1, 3)


def factor_panel(work, hooks):
    strips = LEAF // 8
    sub = lax.broadcasted_iota(jnp.int32, (8, 128), 0)
    for leaf in range(NB // LEAF):
        top = leaf * LEAF
        end = top + LEAF
        tiles = [q for q in range(2) if (q + 1) * 128 > top] + [2 + q for q in range(2) if q * 128 < end]
        rows = {
            (t, q): work[top + 8 * t : top + 8 * t + 8, q * 128 : (q + 1) * 128] for t in range(strips) for q in tiles
        }
        for s in range(strips):
            first = top + 8 * s
            q0, at = first // 128, first % 128
            cols = {
                (i, t): jnp.broadcast_to(rows[t, q0][:, at + i : at + i + 1], (8, 128))
                for i in range(8)
                for t in range(s, strips)
            }
            scales = None
            for i in range(8):
                r = lax.rsqrt(jnp.broadcast_to(cols[i, s][i : i + 1, :], (8, 128)))
                scales = r if scales is None else jnp.where(sub == i, r, scales)
                low = {t: cols[i, t] * r for t in range(s, strips)}
                low[s] = jnp.where(sub > i, low[s], 0.0)
                left = range(s + 1 if i == 7 else s, strips)
                for other in range(i + 1, 8):
                    pivot = jnp.broadcast_to(cols[other, s][i : i + 1, :], (8, 128)) * r
                    for t in left:
                        cols[other, t] = cols[other, t] - low[t] * pivot
                for q in tiles:
                    pivot = jnp.broadcast_to(rows[s, q][i : i + 1, :], (8, 128)) * r
                    for t in left:
                        rows[t, q] = rows[t, q] - low[t] * pivot
            for q in tiles:
                work[first : first + 8, q * 128 : (q + 1) * 128] = rows[s, q] * scales
        if end < NB:
            lo, hi = tiles[0] * 128, (tiles[-1] + 1) * 128
            h, m, l = split3(work[top:end, lo:hi])
            rhs = jnp.concatenate([h, m, h, l, m, h], axis=0)
            lhs = jnp.concatenate([v[:, : NB - lo] for v in (h, h, m, h, m, l)], axis=0)
            prod = lax.dot_general(lhs, rhs, (TN, ((), ())), preferred_element_type=F32)
            work[end:, lo:hi] = work[end:, lo:hi] - prod[end - lo :, :]
        if leaf in hooks:
            hooks[leaf]()


def kernel(
    mat, out, held, aj, lead, ai, uj, li, urow, winv, work,
    local_sem,
    s_sa, s_sj, s_si, s_z, s_al, s_ac, s_j1, s_j2, s_j3, s_iz, s_ic,
    r_sa, r_sj, r_si, r_z, r_al, r_ac, r_j1, r_j2, r_j3, r_iz, r_ic,
):
    row = lax.axis_index("row")
    col = lax.axis_index("col")
    y, x = row // 4, row % 4
    z, core = col // 2, col % 2
    owner = (row == 0) & (col == 0)

    def copy(src, dst, send, recv, **dev):
        return pltpu.make_async_remote_copy(
            src_ref=src, dst_ref=dst, send_sem=send, recv_sem=recv, device_id=dev, device_id_type=MESH
        )

    def wait_here(ref, sem):
        pltpu.make_async_copy(ref, ref, sem).wait()

    def loop(n0, n1, body):
        def step(d, carry):
            body(d)
            return carry

        lax.fori_loop(n0, n1, step, 0)

    def row_at(dy, dx):
        return ((y + dy) % 4) * 4 + (x + dx) % 4

    def col_at(dz):
        return ((z + dz) % 8) * 2 + core

    barrier = pltpu.get_barrier_semaphore()

    def greet(**dev):
        pl.semaphore_signal(barrier, inc=1, device_id=dev, device_id_type=MESH)

    for k in range(PANELS):
        @pl.when(col != k)
        def _():
            greet(col=k)

    loop(1, 16, lambda d: greet(row=(row + d) % 16))
    for d in (1, 2, 6, 7):
        greet(col=col_at(d))
    greet(col=z * 2 + 1 - core)

    load = pltpu.make_async_copy(mat, held, local_sem.at[0])

    lead_at = col * (col + 1) // 2 + row

    def scatter_a(d):
        p = (row + d) % 16
        return copy(
            mat.at[pl.ds(16 * p, 16), pl.ds(0, NB)], lead.at[lead_at, p],
            s_sa.at[d], r_sa.at[row], row=p,
        )

    def scatter_w(p):
        return copy(work.at[pl.ds(16 * p, 16), pl.ds(NB, NB)], lead.at[0, p], s_sa.at[p], r_sa.at[0], row=p)

    def scatter_j(d):
        p = (row + d) % 16
        return copy(mat.at[pl.ds(16 * p, 16), :], aj.at[row, p // 4, p % 4], s_sj.at[d], r_sj.at[row], row=p)

    def scatter_i(d):
        p = (col + d) % 16
        return copy(
            mat.at[pl.ds(64 * p, 64), pl.ds(0, NB)], ai.at[col, p // 2, p % 2], s_si.at[d], r_si.at[col], col=p
        )

    has_lead = (row < PANELS) & (col < PANELS) & (row <= col) & (col > 0)

    def enter():
        pl.semaphore_wait(
            barrier, 20 + 15 * (col < PANELS).astype(jnp.int32)
        )

        @pl.when(has_lead)
        def _():
            pltpu.make_async_copy(
                mat.at[pl.ds(16 * row, 16), pl.ds(0, NB)], lead.at[lead_at, row], r_sa.at[row]
            ).start()
            loop(1, 16, lambda d: scatter_a(d).start())

        @pl.when(col < PANELS)
        def _():
            pltpu.make_async_copy(
                mat.at[pl.ds(64 * col, 64), pl.ds(0, NB)], ai.at[col, z, core], r_si.at[col]
            ).start()
            loop(1, 16, lambda d: scatter_i(d).start())

        @pl.when(row < PANELS)
        def _():
            pltpu.make_async_copy(mat.at[pl.ds(16 * row, 16), :], aj.at[row, y, x], r_sj.at[row]).start()
            loop(1, 16, lambda d: scatter_j(d).start())

    eye = (
        lax.broadcasted_iota(jnp.int32, (NB, NB), 0) == lax.broadcasted_iota(jnp.int32, (NB, NB), 1)
    ).astype(F32)

    @pl.when(owner)
    def _():
        first = pltpu.make_async_copy(mat.at[pl.ds(0, NB), pl.ds(0, NB)], work.at[:, pl.ds(0, NB)], local_sem.at[1])
        first.start()
        first.wait()
        work[:, NB:] = eye
        factor_panel(
            work,
            {
                3: lambda: (enter(), loop(1, 8, lambda p: scatter_w(p).start())),
                4: lambda: loop(8, 10, lambda p: scatter_w(p).start()),
                5: lambda: loop(10, 12, lambda p: scatter_w(p).start()),
                6: lambda: loop(12, 14, lambda p: scatter_w(p).start()),
            },
        )
        loop(14, 16, lambda p: scatter_w(p).start())
        lead[0, 0] = work[:16, NB:]
        load.start()

    @pl.when(jnp.logical_not(owner))
    def _():
        enter()
        load.start()

    def spread(j, d):
        ref = lead.at[pl.ds(FIRST[j], j + 1), row]
        return copy(ref, ref, s_z.at[d], r_z.at[j], col=(col + d) % 16 if j == 0 else col_at(d))

    def relay(j):
        @pl.when(col == j)
        def _():
            if j == 0:
                @pl.when(row > 0)
                def _():
                    wait_here(lead.at[0, row], r_sa.at[0])
            else:
                for k in range(j + 1):
                    wait_here(lead.at[FIRST[j] + k, row], r_sa.at[k])
            loop(1, 8 if j else 16, lambda d: spread(j, d).start())

    def lead_all(j, d):
        ref = lead.at[pl.ds(FIRST[j], j + 1), row]
        return copy(ref, ref, s_al.at[j, d], r_al.at[j, row], row=(row + d) % 16)

    def lead_core(j):
        ref = lead.at[pl.ds(FIRST[j], j + 1)]
        return copy(ref, ref, s_ac.at[j], r_ac.at[j], col=z * 2 + 1 - core)

    def carries(j):
        return core == j % 2 if j else core >= 0

    def send_lead(j):
        @pl.when(carries(j))
        def _():
            @pl.when(col != j)
            def _():
                wait_here(lead.at[pl.ds(FIRST[j], j + 1), row], r_z.at[j])

            loop(1, 16, lambda d: lead_all(j, d).start())

    def gather_lead(j):
        @pl.when(carries(j))
        def _():
            def arrive(d):
                src = (row + d) % 16
                wait_here(lead.at[pl.ds(FIRST[j], j + 1), src], r_al.at[j, src])

            loop(1, 16, arrive)
            if j:
                lead_core(j).start()

    def wait_lead(j):
        @pl.when(core != j % 2)
        def _():
            wait_here(lead.at[pl.ds(FIRST[j], j + 1)], r_ac.at[j])

    HALF = 512
    LOW, HIGH = pl.ds(0, HALF), pl.ds(HALF, HALF)

    def j_first(k, h, d):
        ref = aj.at[k, y, x, :, (LOW, HIGH)[h]]
        if h == 0:
            return copy(ref, ref, s_j1.at[k, h, d], r_j1.at[k, h, x], row=row_at(0, d))
        return copy(ref, ref, s_j1.at[k, h, d], r_j1.at[k, h, y], row=row_at(d, 0))

    def j_group(k, h, at, part):
        inner = (slice(None), pl.ds(0, 2), pl.ds(2, 2))[part]
        if h == 0:
            return aj.at[k, at, inner, :, LOW]
        return aj.at[k, inner, at, :, HIGH]

    def j_dev(h, d):
        return row_at(d, 0) if h == 0 else row_at(0, d)

    def j_mine(h):
        return y if h == 0 else x

    def j_second(k, h, way):
        ref = j_group(k, h, j_mine(h), 0)
        return copy(ref, ref, s_j2.at[k, h, way], r_j2.at[k, h, way], row=j_dev(h, (1, 3)[way]))

    def j_third(k, h, way):
        ref = j_group(k, h, (j_mine(h) + (3, 1)[way]) % 4, 1 + way)
        return copy(ref, ref, s_j3.at[k, h, way], r_j3.at[k, h, way], row=j_dev(h, (1, 3)[way]))

    def bulk_j1(k):
        wait_here(aj.at[k, y, x], r_sj.at[k])
        for h in range(2):
            loop(1, 4, lambda d: j_first(k, h, d).start())

    def bulk_j2(k):
        for h in range(2):
            for d in range(1, 4):
                src = (j_mine(1 - h) + d) % 4
                ref = aj.at[k, y, src, :, LOW] if h == 0 else aj.at[k, src, x, :, HIGH]
                wait_here(ref, r_j1.at[k, h, src])
            for way in range(2):
                j_second(k, h, way).start()

    def bulk_j3(k):
        for h in range(2):
            for way in range(2):
                wait_here(j_group(k, h, (j_mine(h) + (3, 1)[way]) % 4, 0), r_j2.at[k, h, way])
                j_third(k, h, way).start()

    def bulk_j4(k):
        for h in range(2):
            for way in range(2):
                wait_here(j_group(k, h, (j_mine(h) + 2) % 4, 1 + way), r_j3.at[k, h, way])

    STEPS = ((1, 0), (2, 0), (7, 0), (6, 0), (1, 6), (2, 6), (7, 2), (6, 2))

    def i_piece(k, n, at):
        if n == 5:
            return ai.at[k, at, core, pl.ds(0, 32)]
        if n == 7:
            return ai.at[k, at, core, pl.ds(32, 32)]
        return ai.at[k, at, core]

    def i_ring(k, n):
        far, whose = STEPS[n]
        ref = i_piece(k, n, (z + whose) % 8)
        return copy(ref, ref, s_iz.at[k, n], r_iz.at[k, n], col=col_at(far))

    def i_arrive(k, n):
        far, whose = STEPS[n]
        wait_here(i_piece(k, n, (z + whose + 8 - far) % 8), r_iz.at[k, n])

    def i_core(k, at):
        ref = ai.at[k, at % 8, core]
        return copy(ref, ref, s_ic.at[k, at % 8], r_ic.at[k, at % 8], col=z * 2 + 1 - core)

    def bulk_i(k, step):
        if step == 0:
            wait_here(ai.at[k, z, core], r_si.at[k])
            for n in range(4):
                i_ring(k, n).start()
            i_core(k, z).start()
        elif step == 1:
            for n in (1, 3):
                i_arrive(k, n)
            for n in range(4, 8):
                i_ring(k, n).start()
            for n in (0, 2):
                i_arrive(k, n)
            for at in (1, 2, 6, 7):
                i_core(k, z + at).start()
        else:
            for n in range(4, 8):
                i_arrive(k, n)
            for at in (3, 4, 5):
                i_core(k, z + at).start()

    def bulk_i_end(k):
        loop(0, 8, lambda at: wait_here(ai.at[k, at, 1 - core], r_ic.at[k, at]))

    def each(f, *args):
        for k in range(PANELS):
            f(k, *args)

    relay(1)
    relay(2)
    relay(0)
    send_lead(1)
    send_lead(2)
    each(bulk_i, 0)
    send_lead(0)
    gather_lead(1)
    each(bulk_j1)
    gather_lead(0)

    hooks = [
        {},
        {
            0: lambda: each(bulk_i, 1),
            2: lambda: gather_lead(2),
            4: lambda: each(bulk_j2),
        },
        {
            0: lambda: each(bulk_i, 2),
            2: lambda: each(bulk_j3),
        },
    ]

    @pl.when(owner)
    def _():
        loop(1, 16, lambda p: scatter_w(p).wait_send())

    def block(kk, j):
        return split3(urow[kk, :, NB * (j - 1) : NB * j])

    for k in range(PANELS):
        if k == 0:
            wait_lead(1)
            winv[0] = lead[0].reshape(NB, NB)
        else:
            if k == 2:
                wait_lead(2)
                urow[0, :, NB:] = dot_parts(split3(winv[0]), split3(lead[3].reshape(NB, NB)), NN)
                t = lead[4].reshape(NB, NB) - dot_parts(block(0, 1), block(0, 2), TN)
                urow[1, :, NB:] = dot_parts(split3(winv[1]), split3(t), NN)
            diag = lead[FIRST[k] + k].reshape(NB, NB)
            for kk in range(k):
                u = block(kk, k)
                diag = diag - dot_parts(u, u, TN)
            work[:, :NB] = diag
            work[:, NB:] = eye
            factor_panel(work, hooks[k])
            winv[k] = work[:, NB:]
        if k == 0:
            urow[0, :, :NB] = dot_parts(split3(winv[0]), split3(lead[1].reshape(NB, NB)), NN)

    for k in range(PANELS):
        bulk_j4(k)
        bulk_i_end(k)
        inv = split3(winv[k])
        for ch in range(4):
            at = slice(NB * ch, NB * ch + NB)
            rhs = aj[k, :, :, :, at].reshape(NB, NB)
            lhs = ai[k, 2 * ch : 2 * ch + 2].reshape(NB, NB)
            for kk in range(k):
                u = block(kk, k)
                rhs = rhs - dot_parts(u, [uj[kk, i, :, at] for i in range(3)], TN)
                lhs = lhs - dot_parts([li[kk, i, at] for i in range(3)], u, NN)
            for i, part in enumerate(split3(dot_parts(inv, split3(rhs), NN))):
                uj[k, i, :, at] = part
            for i, part in enumerate(split3(dot_parts(split3(lhs), inv, NT))):
                li[k, i, at] = part

    load.wait()

    for ch in range(4):
        at = slice(NB * ch, NB * ch + NB)
        for cc in range(4):
            to = slice(NB * cc, NB * cc + NB)
            lhs = jnp.concatenate([li[k, i, at] for k in range(PANELS) for i in LEFT], axis=1)
            rhs = jnp.concatenate([uj[k, i, :, to] for k in range(PANELS) for i in RIGHT], axis=0)
            held[at, to] = held[at, to] - jnp.dot(lhs, rhs, preferred_element_type=F32)

    @pl.when(row < PANELS)
    def _():
        held[:NB, :] = jnp.zeros((NB, 4 * NB), F32)

    rr = lax.broadcasted_iota(jnp.int32, (NB, NB), 0)
    cc = lax.broadcasted_iota(jnp.int32, (NB, NB), 1)

    def joined(k, at):
        return li[k, 0, at].astype(F32) + (li[k, 1, at].astype(F32) + li[k, 2, at].astype(F32))

    for k in range(PANELS):
        @pl.when(col == k)
        def _():
            keep = (row > k) | ((row == k) & (rr >= cc))
            held[:NB, :NB] = jnp.where(keep, joined(k, slice(0, NB)), 0.0)
            held[NB:, :NB] = joined(k, slice(NB, 4 * NB))

    store = pltpu.make_async_copy(held, out, local_sem.at[1])
    store.start()

    @pl.when(has_lead)
    def _():
        loop(1, 16, lambda d: scatter_a(d).wait_send())

    @pl.when(row < PANELS)
    def _():
        loop(1, 16, lambda d: scatter_j(d).wait_send())

    @pl.when(col < PANELS)
    def _():
        loop(1, 16, lambda d: scatter_i(d).wait_send())

    for j in range(PANELS):
        @pl.when(col == j)
        def _():
            loop(1, 8 if j else 16, lambda d: spread(j, d).wait_send())

        @pl.when(carries(j))
        def _():
            loop(1, 16, lambda d: lead_all(j, d).wait_send())
            if j:
                lead_core(j).wait_send()

    for k in range(PANELS):
        for h in range(2):
            loop(1, 4, lambda d: j_first(k, h, d).wait_send())
            for way in range(2):
                j_second(k, h, way).wait_send()
                j_third(k, h, way).wait_send()
        for n in range(8):
            i_ring(k, n).wait_send()
        loop(0, 8, lambda at: i_core(k, at).wait_send())
    store.wait()


def body(matrix):
    rows = matrix.shape[0]
    dma = pltpu.SemaphoreType.DMA
    sent = [(16,), (16,), (16,), (16,), (3, 16), (3,), (3, 2, 4), (3, 2, 2), (3, 2, 2), (3, 8), (3, 8)]
    landed = [(3,), (3,), (3,), (3,), (3, 16), (3,), (3, 2, 4), (3, 2, 2), (3, 2, 2), (3, 8), (3, 8)]
    return pl.pallas_call(
        kernel,
        out_shape=jax.ShapeDtypeStruct(matrix.shape, F32),
        in_specs=[pl.BlockSpec(memory_space=pl.ANY)],
        out_specs=pl.BlockSpec(memory_space=pl.ANY),
        scratch_shapes=[
            pltpu.VMEM(matrix.shape, F32),
            pltpu.VMEM((PANELS, 4, 4, 16, rows), F32),
            pltpu.VMEM((6, 16, 16, NB), F32),
            pltpu.VMEM((PANELS, 8, 2, 64, NB), F32),
            pltpu.VMEM((PANELS, 3, NB, rows), BF16),
            pltpu.VMEM((PANELS, 3, rows, NB), BF16),
            pltpu.VMEM((PANELS - 1, NB, (PANELS - 1) * NB), F32),
            pltpu.VMEM((PANELS, NB, NB), F32),
            pltpu.VMEM((NB, 2 * NB), F32),
            dma((2,)),
        ]
        + [dma(g) for g in sent]
        + [dma(g) for g in landed],
        compiler_params=pltpu.CompilerParams(
            collective_id=0, has_side_effects=True, vmem_limit_bytes=56 * 1024 * 1024
        ),
    )(matrix)


def solution(mesh):
    return jax.shard_map(body, mesh=mesh, in_specs=(P("row", "col"),), out_specs=P("row", "col"), check_vma=False)
```

time: 115 us -> 93.7 us (0.81); the launches traced: 114 us -> 93.6 us
  Pallas kernels: 109 us -> 88.8 us
    pallas_call x1, Pallas kernels: 109 us -> 88.8 us  [body(): pl.pallas_call(kernel, out_shape=jax.ShapeDtypeStruct(matrix.shape, F32),...]
where the time goes in v2:
time: 93.7 us; the launch traced here: 93.6 us
  Pallas kernels  88.8 us (95%)
  local copies, waits for them, and re-layouts  4.79 us (5%)
    pallas_call x1, Pallas kernels, body(): pl.pallas_call(kernel, out_shape=jax.ShapeDtypeStruct(matrix.shape, F32),...  88.8 us
    unnamed x1, local copies, waits for them, and re-layouts  4.79 us

profile of v2, /device:TPU:1, one launch (start us, length us, event | category | flops | bytes accessed | tf_op | source)
XLA Modules:
  0.0 93.6 jit_solution(6270519294296925780)
XLA Ops:
  0.0 88.8 %shard_map.17 = f32[1024,1024]{1,0:T(8,128)} custom-call(f32[1024,1024]{1,0:T(8,128)} %mat.1), custom_call_target="tpu_custom_call" | custom-call | tf_op jit(solution)/shard_map/pallas_call | solution.py:508
  88.8 4.8 %copy.3 = f32[1024,1024]{1,0:T(8,128)} copy(f32[1024,1024]{1,0:T(8,128)} %shard_map.17) | data formatting | bytes 8388608

commit v3 on v2

--- a/solution.py
+++ b/solution.py
@@ -437,6 +437,13 @@
 
     load.wait()
 
+    rr = lax.broadcasted_iota(jnp.int32, (NB, NB), 0)
+    cols_at = lax.broadcasted_iota(jnp.int32, (NB, NB), 1)
+
+    def store(ch):
+        band = pl.ds(NB * ch, NB)
+        return pltpu.make_async_copy(held.at[band], out.at[band], local_sem.at[2 + ch])
+
     for ch in range(4):
         at = slice(NB * ch, NB * ch + NB)
         for cc in range(4):
@@ -444,26 +451,20 @@
             lhs = jnp.concatenate([li[k, i, at] for k in range(PANELS) for i in LEFT], axis=1)
             rhs = jnp.concatenate([uj[k, i, :, to] for k in range(PANELS) for i in RIGHT], axis=0)
             held[at, to] = held[at, to] - jnp.dot(lhs, rhs, preferred_element_type=F32)
-
-    @pl.when(row < PANELS)
-    def _():
-        held[:NB, :] = jnp.zeros((NB, 4 * NB), F32)
-
-    rr = lax.broadcasted_iota(jnp.int32, (NB, NB), 0)
-    cc = lax.broadcasted_iota(jnp.int32, (NB, NB), 1)
-
-    def joined(k, at):
-        return li[k, 0, at].astype(F32) + (li[k, 1, at].astype(F32) + li[k, 2, at].astype(F32))
-
-    for k in range(PANELS):
-        @pl.when(col == k)
-        def _():
-            keep = (row > k) | ((row == k) & (rr >= cc))
-            held[:NB, :NB] = jnp.where(keep, joined(k, slice(0, NB)), 0.0)
-            held[NB:, :NB] = joined(k, slice(NB, 4 * NB))
-
-    store = pltpu.make_async_copy(held, out, local_sem.at[1])
-    store.start()
+        if ch == 0:
+            @pl.when(row < PANELS)
+            def _():
+                held[:NB, :] = jnp.zeros((NB, 4 * NB), F32)
+
+        for k in range(PANELS):
+            @pl.when(col == k)
+            def _():
+                value = li[k, 0, at].astype(F32) + (li[k, 1, at].astype(F32) + li[k, 2, at].astype(F32))
+                if ch == 0:
+                    value = jnp.where((row > k) | ((row == k) & (rr >= cols_at)), value, 0.0)
+                held[at, :NB] = value
+
+        store(ch).start()
 
     @pl.when(has_lead)
     def _():
@@ -497,7 +498,8 @@
         for n in range(8):
             i_ring(k, n).wait_send()
         loop(0, 8, lambda at: i_core(k, at).wait_send())
-    store.wait()
+    for ch in range(4):
+        store(ch).wait()
 
 
 def body(matrix):
@@ -520,7 +522,7 @@
             pltpu.VMEM((PANELS - 1, NB, (PANELS - 1) * NB), F32),
             pltpu.VMEM((PANELS, NB, NB), F32),
             pltpu.VMEM((NB, 2 * NB), F32),
-            dma((2,)),
+            dma((6,)),
         ]
         + [dma(g) for g in sent]
         + [dma(g) for g in landed],

time: 93.7 us -> 93.5 us (level)
  no operation moved by 1% of the time
where the time goes in v3:
time: 93.5 us; the launch traced here: 93.4 us
  Pallas kernels  88.6 us (95%)
  local copies, waits for them, and re-layouts  4.79 us (5%)
    pallas_call x1, Pallas kernels, body(): pl.pallas_call(kernel, out_shape=jax.ShapeDtypeStruct(matrix.shape, F32),...  88.6 us
    unnamed x1, local copies, waits for them, and re-layouts  4.79 us

profile of v3, /device:TPU:1, one launch (start us, length us, event | category | flops | bytes accessed | tf_op | source)
XLA Modules:
  0.0 93.4 jit_solution(17709296898717722424)
XLA Ops:
  0.0 88.6 %shard_map.17 = f32[1024,1024]{1,0:T(8,128)} custom-call(f32[1024,1024]{1,0:T(8,128)} %mat.1), custom_call_target="tpu_custom_call" | custom-call | tf_op jit(solution)/shard_map/pallas_call | solution.py:510
  88.6 4.8 %copy.3 = f32[1024,1024]{1,0:T(8,128)} copy(f32[1024,1024]{1,0:T(8,128)} %shard_map.17) | data formatting | bytes 8388608
